TPU v7x, 32 devices: a whole 2x2x4 slice. The times are simulated.
32 devices in a mesh: groups: 2 (over y), expert: 4 (over z), dp: 2 (over x), mp: 2 (over core).
Axes of the slice: x: 2, y: 2, z: 4, core: 2. Of those that a mesh axis runs over, the one named last changes fastest.
Arguments:
- hidden: bfloat16 [1024, 2048], P(('groups', 'expert', 'dp'), 'mp'), parts along dimension 0, may hold values from -6 to 6
- queries: bfloat16 [1024, 2048], P(('groups', 'expert', 'dp'), 'mp'), parts along dimension 0, may hold values from -6 to 120
- memory: bfloat16 [1024, 2, 2048], P(('groups', 'expert', 'dp'), None, 'mp'), parts along dimension 0, may hold values from -6 to 40.5
- target_pair: int32 [1024], P(('groups', 'expert', 'dp')), parts along dimension 0, may hold values from 0 to 15, as said below
- source_pair: int32 [1024], P(('groups', 'expert', 'dp')), parts along dimension 0, may hold values from 0 to 15, as said below
- routes: int32 [1024, 2], P(('groups', 'expert', 'dp')), parts along dimension 0, may hold values from 0 to 3, all different within a row; in each aligned block of 64 rows (0 to 63, 64 to 127, ...) at most 40 rows name the same one
- route_weight: float32 [1024, 2], P(('groups', 'expert', 'dp')), parts along dimension 0, may hold values from 0.1 to 1
- norm_gain: float32 [2048], replicated, may hold values from 0.5 to 1.5
- norm_bias: float32 [2048], replicated, may hold values from -3 to 3
- expert_in: bfloat16 [4, 2048, 8192], P('expert', None, ('dp', 'mp')), may hold values from -0.125 to 0.125
- expert_out: bfloat16 [4, 8192, 2048], P('expert', ('dp', 'mp')), may hold values from -0.0625 to 0.0625
Outputs:
- mixed: bfloat16 [1024, 2048], P(('groups', 'expert', 'dp'), 'mp'), parts along dimension 0
There are 2 independent parts, one for each index of `groups`. A program takes and returns all parts, laid end to end along the dimension named above; an argument that names none is the same for every part. Nothing has to cross between parts.
Inputs may be any that keep to these rules, and one draw needn't show every extreme that they name: `target_pair`: within each batch pair numbers run over 0 to 15; each pair's target tokens form one contiguous run on one index of expert and dp, which holds the tokens of 4 pairs. `source_pair`: within each batch, memory rows read by expert index and then row carry pair numbers that never fall, and every pair has at least one row. `routes`: among the rows of one device no expert is named more than 40 times.
All inputs are finite; a program needn't handle non-finite values.
Results may differ from a plain program's by a relative error of at most 0.008.
Values may be sent and summed in bfloat16 or wider, within the bound.
A program may use at most 128 MiB of HBM per device.

v0:
```python
import math

import jax
import jax.numpy as jnp
from jax import lax
from jax.sharding import PartitionSpec as P

HEAD = 128


EPSILON = 1e-05
NEGATIVE = -1e30


def shards(
    hidden,
    queries,
    memory,
    target_pair,
    source_pair,
    routes,
    route_weight,
    norm_gain,
    norm_bias,
    expert_in,
    expert_out,
):
    tok_rows = hidden.shape[0]
    local_heads = queries.shape[1] // HEAD
    scale = 1.0 / math.sqrt(HEAD)
    query_heads = queries.reshape(tok_rows, local_heads, HEAD)
    running = jnp.full((local_heads, tok_rows), NEGATIVE, jnp.float32)
    rows = lax.all_gather(memory, "expert", axis=0, tiled=True)
    row_pairs = lax.all_gather(source_pair, "expert", axis=0, tiled=True)
    count = rows.shape[0]
    keys = rows[:, 0, :].reshape(count, local_heads, HEAD)
    values = rows[:, 1, :].reshape(count, local_heads, HEAD)
    score = (
        jnp.einsum("thd,rhd->htr", query_heads, keys, preferred_element_type=jnp.float32) * scale
    )
    match = (target_pair[:, None] == row_pairs[None, :])[None]
    masked = jnp.where(match, score, NEGATIVE)
    newest = jnp.maximum(running, jnp.max(masked, axis=-1))
    weight = jnp.where(match, jnp.exp(masked - newest[:, :, None]), 0.0)
    total = jnp.sum(weight, axis=-1)
    summed = jnp.einsum(
        "htr,rhd->htd", weight.astype(jnp.bfloat16), values, preferred_element_type=jnp.float32
    )
    running, total, summed = (newest, total, summed)
    context = jnp.transpose(summed / total[:, :, None], (1, 0, 2)).reshape(
        tok_rows, local_heads * HEAD
    )
    attended = (hidden.astype(jnp.float32) + context).astype(jnp.bfloat16)
    full_rows = lax.all_gather(attended, "mp", axis=1, tiled=True)
    width = full_rows.shape[1]
    experts_all = lax.axis_size("expert")
    batches = lax.axis_size("dp")
    cap = 2 * tok_rows // experts_all * 5 // 4
    flat = routes.reshape(-1)
    named = (flat[:, None] == jnp.arange(experts_all, dtype=jnp.int32)[None, :]).astype(jnp.int32)
    slot = jnp.sum((jnp.cumsum(named, axis=0) - named) * named, axis=1)
    dest = flat * cap + slot
    place = dest[:, None] == jnp.arange(experts_all * cap, dtype=jnp.int32)[None, :]
    per_token = jnp.sum(place.reshape(tok_rows, 2, experts_all * cap).astype(jnp.bfloat16), axis=1)
    outgoing = lax.dot_general(
        per_token, full_rows, (((0,), (0,)), ((), ())), preferred_element_type=jnp.float32
    ).astype(jnp.bfloat16)
    copies = jnp.broadcast_to(
        outgoing.reshape(experts_all, 1, cap, width), (experts_all, batches, cap, width)
    ).reshape(experts_all * batches * cap, width)
    arrived = lax.all_to_all(copies, ("expert", "dp"), split_axis=0, concat_axis=0, tiled=True)
    values = arrived.astype(jnp.float32)
    center = jnp.mean(values, axis=-1, keepdims=True)
    spread = jnp.mean(jnp.square(values - center), axis=-1, keepdims=True)
    normed = ((values - center) * lax.rsqrt(spread + EPSILON) * norm_gain + norm_bias).astype(
        jnp.bfloat16
    )
    active = jax.nn.relu(jnp.dot(normed, expert_in[0], preferred_element_type=jnp.float32)).astype(
        jnp.bfloat16
    )
    partial_value = jnp.dot(active, expert_out[0], preferred_element_type=jnp.float32).astype(
        jnp.bfloat16
    )
    returned = lax.all_to_all(
        partial_value, ("expert", "dp"), split_axis=0, concat_axis=0, tiled=True
    )
    expert_sum = jnp.sum(
        returned.reshape(experts_all, batches, cap, width).astype(jnp.float32), axis=1
    )
    picked = jnp.dot(
        place.astype(jnp.float32),
        expert_sum.reshape(experts_all * cap, width),
        precision=lax.Precision.HIGHEST,
    )
    blended = jnp.sum(picked.reshape(tok_rows, 2, width) * route_weight[:, :, None], axis=1)
    share = lax.psum_scatter(
        blended.astype(jnp.bfloat16), "mp", scatter_dimension=1, tiled=True
    ).astype(jnp.float32)
    return (attended.astype(jnp.float32) + share).astype(jnp.bfloat16)


def solution(mesh):
    return jax.shard_map(
        shards,
        mesh=mesh,
        in_specs=(
            P(("groups", "expert", "dp"), "mp"),
            P(("groups", "expert", "dp"), "mp"),
            P(("groups", "expert", "dp"), None, "mp"),
            P(("groups", "expert", "dp")),
            P(("groups", "expert", "dp")),
            P(("groups", "expert", "dp"), None),
            P(("groups", "expert", "dp"), None),
            P(),
            P(),
            P("expert", None, ("dp", "mp")),
            P("expert", ("dp", "mp"), None),
        ),
        out_specs=P(("groups", "expert", "dp"), "mp"),
        check_vma=False,
    )
```

profile of v0, /device:TPU:0, one launch (start us, length us, event | category | flops | bytes accessed | tf_op | source)
XLA Modules:
  0.0 148.1 jit_solution(10495505063601206719)
XLA Ops:
  6.5 0.7 all-gather.2.cloned.1.call-update
  7.3 0.8 copy.53
  8.9 1.3 dynamic-slice
  10.8 0.9 dynamic-update-slice
  11.7 9.9 %all-reduce = s32[256]{0:T(256)S(1)} all-reduce(s32[256]{0:T(256)S(1)} %dynamic-update-slice), channel_id=1, replica_groups=mesh['groups'=2,'expert'=4,'dp'=2,'mp'=2] {'expert'}, use_global_device_ids=true, to_apply=%add | all-reduce | flops 256 | bytes 2048
  21.6 0.7 multiply_add_fusion
  22.4 0.7 broadcast_compare_fusion
  23.1 16.5 %all-gather.2.cloned.1.call-done = bf16[256,2,1024]{2,1,0:T(2,128)(2,1)} async-done(((bf16[64,2,1024]{2,1,0:T(2,128)(2,1)}), bf16[256,2,1024]{2,1,0:T(2,128)(2,1)}) %all-gather.2.cloned.1.call-update) | async-done | bytes 1048592 | tf_op jit(solution)/shard_map/all_gather | solution.py:33
  39.6 3.2 %fusion.42 = (bf16[256,1,1024]{2,1,0:T(2,128)(2,1)S(1)}, bf16[256,1,1024]{2,1,0:T(2,128)(2,1)S(1)}) fusion(bf16[256,2,1024]{2,1,0:T(2,128)(2,1)} %all-gather.2.cloned.1.call-done), kind=kLoop, calls=%fused_computation.51 | loop fusion | bytes 2097152 | tf_op jit(solution)/shard_map/slice | solution.py:36
  42.9 0.9 copy.57
  43.8 0.3 fusion.43
  44.2 0.9 copy.58
  45.1 0.3 fusion.25
  45.4 0.3 fusion.22
  45.8 2.0 %all_gather.11 = bf16[64,2048]{1,0:T(8,128)(2,1)S(1)} all-gather(bf16[64,1024]{1,0:T(8,128)(2,1)S(1)} %fusion.28), channel_id=1, replica_groups=mesh['groups'=2,'expert'=4,'dp'=2,'mp'=2] {'mp'}, dimensions={1}, use_global_device_ids=true | all-gather | bytes 393216 | tf_op jit(solution)/shard_map/all_gather | solution.py:54
  47.7 0.3 convolution_convert_fusion
  48.3 35.6 %all_to_all.18 = bf16[8,40,2048]{2,1,0:T(8,128)(2,1)S(1)} all-to-all(bf16[8,40,2048]{2,1,0:T(8,128)(2,1)S(1)} %bitcast.59), channel_id=1, replica_groups=mesh['groups'=2,'expert'=4,'dp'=2,'mp'=2] {'expert','dp'}, dimensions={0} | all-to-all | bytes 2621440 | tf_op jit(solution)/shard_map/all_to_all | solution.py:71
  84.1 0.5 fusion.15
  84.6 0.6 fusion.18
  85.2 11.3 %fusion.12 = bf16[320,2048]{1,0:T(8,128)(2,1)S(1)} fusion(bf16[1,2048,2048]{2,1,0:T(8,128)(2,1)} %param.21, bf16[320,2048]{1,0:T(8,128)(2,1)S(1)} %bitcast.62, bf16[1,2048,2048]{2,1,0:T(8,128)(2,1)} %param.20), kind=kOutput, calls=%fused_computation.10 | convolution fusion | flops 5370675200 | bytes 19398656 | tf_op jit(solution)/shard_map/dot_general | solution.py:81
  96.5 34.5 %all_to_all.19 = bf16[8,40,2048]{2,1,0:T(8,128)(2,1)S(1)} all-to-all(bf16[8,40,2048]{2,1,0:T(8,128)(2,1)S(1)} %bitcast.63), channel_id=1, replica_groups=mesh['groups'=2,'expert'=4,'dp'=2,'mp'=2] {'expert','dp'}, dimensions={0} | all-to-all | bytes 2621440 | tf_op jit(solution)/shard_map/all_to_all | solution.py:84
  131.3 1.5 fusion.19
  132.8 6.8 %reduce-scatter.2.cloned.1.call-done = bf16[64,1024]{1,0:T(8,128)(2,1)} async-done(((bf16[64,2048]{1,0:T(8,128)(2,1)}), bf16[64,1024]{1,0:T(8,128)(2,1)}) %reduce-scatter.2.cloned.1.call-update) | async-done | bytes 131088 | tf_op jit(solution)/shard_map/reduce_scatter | solution.py:96
  139.6 1.6 %add_convert_fusion = bf16[64,1024]{1,0:T(8,128)(2,1)} fusion(bf16[64,1024]{1,0:T(8,128)(2,1)} %reduce-scatter.2.cloned.1.call-done, bf16[64,1024]{1,0:T(8,128)(2,1)S(1)} %fusion.28), kind=kLoop, calls=%fused_computation.29 | loop fusion | flops 262144 | bytes 393216 | tf_op jit(solution)/shard_map/convert_element_type | solution.py:99
  (28 shorter events, 1.6 us)
Async XLA Ops:
  6.5 37.3 %copy-start = (bf16[64,1024]{1,0:T(8,128)(2,1)S(1)}, bf16[64,1024]{1,0:T(8,128)(2,1)}, u32[]{:S(2)}) copy-start(bf16[64,1024]{1,0:T(8,128)(2,1)} %param.12) | copy-start | bytes 393220
  6.5 33.1 %all-gather.2.cloned.1.call-start = ((), (), s32[]{:S(2)}) async-start(), calls=%async_computation.3 | async-start | bytes 1310720 | tf_op jit(solution)/shard_map/all_gather | solution.py:33
  7.3 132.4 %reduce-scatter.2.cloned.1.call-start = ((), (), s32[]{:S(2)}) async-start(), calls=%async_computation.4 | async-start | bytes 393216 | tf_op jit(solution)/shard_map/reduce_scatter | solution.py:96
  43.8 1.9 %copy-start.1 = (bf16[64,1024]{1,0:T(8,128)(2,1)S(1)}, bf16[64,1024]{1,0:T(8,128)(2,1)}, u32[]{:S(2)}) copy-start(bf16[64,1024]{1,0:T(8,128)(2,1)} %param.11) | copy-start | bytes 393220
  48.3 36.3 %copy-start.2 = (f32[2048]{0:T(1024)S(1)}, f32[2048]{0:T(1024)}, u32[]{:S(2)}) copy-start(f32[2048]{0:T(1024)} %param.19) | copy-start | bytes 24580
  48.3 36.3 %copy-start.3 = (f32[2048]{0:T(1024)S(1)}, f32[2048]{0:T(1024)}, u32[]{:S(2)}) copy-start(f32[2048]{0:T(1024)} %param.18) | copy-start | bytes 24580
  96.5 34.8 %copy-start.4 = (f32[64,2]{0,1:T(2,128)S(1)}, f32[64,2]{0,1:T(2,128)}, u32[]{:S(2)}) copy-start(f32[64,2]{0,1:T(2,128)} %param.17) | copy-start | bytes 1540
Sparse Core Ops, SparseCore 0:
  8.9 30.6 all-gather.1
  132.9 6.6 reduce-scatter.1
where the time goes:
time: 148 us
  blocking collectives  82 us (55%)
  waiting for transfers between devices  24.1 us (16%)
  between operations  14.3 us (10%)
  matrix products  13.8 us (9%)
  local copies, waits for them, and re-layouts  8.49 us (6%)
  other arithmetic  5.38 us (4%)
    all_to_all x1, blocking collectives, shards(): lax.all_to_all(copies, ('expert', 'dp'), split_axis=0, concat_axis=0, til...  35.6 us
    all_to_all x1, blocking collectives, shards(): lax.all_to_all(partial_value, ('expert', 'dp'), split_axis=0, concat_axis...  34.5 us
    all_gather x1, waiting for transfers between devices, shards(): rows = lax.all_gather(memory, 'expert', axis=0, tiled=True)  16.5 us
    dot_general x1, matrix products, shards(): jnp.dot(active, expert_out[0], preferred_element_type=jnp.float32)  11.3 us
    unnamed x1, blocking collectives  9.92 us
    reduce_scatter x1, waiting for transfers between devices, shards(): lax.psum_scatter(blended.astype(jnp.bfloat16), 'mp', scatter_dimension=1,...  6.83 us
    unnamed x16, local copies, waits for them, and re-layouts  4.74 us
    slice x1, local copies, waits for them, and re-layouts, shards(): keys = rows[:, 0, :].reshape(count, local_heads, HEAD)  3.25 us
  transfers between devices with their start and end apart: 2, of which 2 were waited for; matrix products, arithmetic and copies ran while one was open for 3% of the time, Pallas kernels for 0%

commit v1 on v0

v1 whole, which is shorter than its diff:
```python
import functools
import math

import jax
import jax.numpy as jnp
from jax import lax
from jax.experimental import pallas as pl
from jax.experimental.pallas import tpu as pltpu
from jax.sharding import PartitionSpec as P

HEAD = 128
EPSILON = 1e-05
NEGATIVE = -1e30
MESH = pl.DeviceIdType.MESH
F32 = jnp.float32
BF16 = jnp.bfloat16


def remote(src, dst, send, recv, **where):
    return pltpu.make_async_remote_copy(
        src_ref=src, dst_ref=dst, send_sem=send, recv_sem=recv, device_id=where, device_id_type=MESH
    )


def layer(
    E, DP, NC, NQ, C,
    kv_ref, sp_ref, q_ref, hid_ref, tp_ref, routes_ref, rw_ref, gain_ref, bias_ref, w1_hbm, w2_hbm,
    out_ref,
    kv, sp, w1, w2, att, stat_out, stat_in, sendbuf, xbuf, act, psend, pown, prec, xs, xr, zs, zr,
    wsem, lsem, kv_send, kv_recv, sp_send, sp_recv, st_send, st_recv,
    dz_send, dz_recv, dx_send, dx_recv, dp_send, dp_recv,
    rp_send, rp_recv, rx_send, rx_recv, rz_send, rz_recv,
):
    z = lax.axis_index("expert")
    x = lax.axis_index("dp")
    m = lax.axis_index("mp")
    T, W = q_ref.shape
    other = 1 - m
    S = sp_ref.shape[1]
    cols = W // NC
    wq = W // NQ
    FFL = w1.shape[1]
    EC = E * C

    copies_w = [
        pltpu.make_async_copy(w1_hbm, w1, wsem.at[0]),
        pltpu.make_async_copy(w2_hbm, w2, wsem.at[1]),
    ]
    own_kv = pltpu.make_async_copy(kv_ref, kv.at[z], lsem.at[0])
    own_kv.start()

    barrier = pltpu.get_barrier_semaphore()
    for d in range(1, E):
        pl.semaphore_signal(
            barrier, inc=1, device_id={"expert": lax.rem(z + d, E)}, device_id_type=MESH
        )
    for k in range(1, DP):
        pl.semaphore_signal(
            barrier, inc=1, device_id={"dp": lax.rem(x + k, DP)}, device_id_type=MESH
        )
    pl.semaphore_signal(barrier, inc=1, device_id={"mp": other}, device_id_type=MESH)
    pl.semaphore_wait(barrier, E - 1 + DP - 1 + 1)

    def hop(direction, h, c):
        owner = z - h if direction == 0 else z + h
        target = z + 1 if direction == 0 else z - 1
        src = kv_ref.at[c] if h == 0 else kv.at[owner, c]
        return remote(
            src, kv.at[owner, c], kv_send.at[direction, h, c], kv_recv.at[direction, h, c], expert=target
        )

    def sends(direction, h):
        if direction == 0:
            return jnp.logical_and(z >= h, z < E - 1)
        return jnp.logical_and(z <= E - 1 - h, z > 0)

    def arrived(direction, h, c):
        owner = z - h if direction == 0 else z + h
        return remote(
            kv.at[owner, c], kv.at[owner, c],
            kv_send.at[direction, h - 1, c], kv_recv.at[direction, h - 1, c], expert=owner,
        )

    for c in range(NC):
        for direction in range(2):
            @pl.when(sends(direction, 0))
            def _():
                hop(direction, 0, c).start()

    sp_copies = []
    for d in range(1, E):
        copy = remote(
            sp_ref, sp.at[z], sp_send.at[d - 1], sp_recv.at[d - 1], expert=lax.rem(z + d, E)
        )
        copy.start()
        sp_copies.append(copy)
    for copy in copies_w:
        copy.start()

    r0 = routes_ref[:, 0:1]
    r1 = routes_ref[:, 1:2]
    lane = lax.broadcasted_iota(jnp.int32, (T, 128), 1)
    member = jnp.logical_or(lane == r0, lane == r1).astype(F32).astype(BF16)
    tri = (
        lax.broadcasted_iota(jnp.int32, (T, T), 0) > lax.broadcasted_iota(jnp.int32, (T, T), 1)
    ).astype(F32).astype(BF16)
    slots = jnp.dot(tri, member, preferred_element_type=F32)
    slot0 = jnp.sum(jnp.where(lane == r0, slots, 0.0), axis=1, keepdims=True).astype(jnp.int32)
    slot1 = jnp.sum(jnp.where(lane == r1, slots, 0.0), axis=1, keepdims=True).astype(jnp.int32)
    place_lane = lax.broadcasted_iota(jnp.int32, (T, EC), 1)
    place0 = place_lane == r0 * C + slot0
    place1 = place_lane == r1 * C + slot1
    place = jnp.logical_or(place0, place1).astype(F32).astype(BF16)
    mixing = jnp.where(place0, rw_ref[:, 0:1], 0.0) + jnp.where(place1, rw_ref[:, 1:2], 0.0)
    mix_hi = mixing.astype(BF16)
    mix_lo = (mixing - mix_hi.astype(F32)).astype(BF16)

    for h in range(1, E):
        for c in range(NC):
            for direction in range(2):
                here = z >= h if direction == 0 else z <= E - 1 - h

                @pl.when(here)
                def _():
                    arrived(direction, h, c).wait_recv()

                if h < E - 1:
                    @pl.when(sends(direction, h))
                    def _():
                        hop(direction, h, c).start()
    own_kv.wait()
    for copy in sp_copies:
        copy.wait_recv()

    tp = tp_ref[...]
    match = jnp.concatenate(
        [jnp.where(j == z, sp_ref[...], sp[j]) for j in range(E)], axis=1
    ) == tp
    scale = 1.0 / math.sqrt(HEAD)
    for c in range(NC):
        for n in range(cols // HEAD):
            at = slice(n * HEAD, (n + 1) * HEAD)
            full = slice(c * cols + n * HEAD, c * cols + (n + 1) * HEAD)
            keys = kv[:, c, 0, :, at].reshape(E * S, HEAD)
            vals = kv[:, c, 1, :, at].reshape(E * S, HEAD)
            score = lax.dot_general(
                q_ref[:, full], keys, (((1,), (1,)), ((), ())), preferred_element_type=F32
            ) * scale
            masked = jnp.where(match, score, NEGATIVE)
            largest = jnp.max(masked, axis=1, keepdims=True)
            weight = jnp.where(match, jnp.exp(masked - largest), 0.0)
            total = jnp.sum(weight, axis=1, keepdims=True)
            context = jnp.dot(weight.astype(BF16), vals, preferred_element_type=F32) / total
            att[:, full] = (hid_ref[:, full].astype(F32) + context).astype(BF16)

    rows = att[...].astype(F32)
    mean = jnp.mean(rows, axis=1, keepdims=True)
    dev = rows - mean
    m2 = jnp.sum(dev * dev, axis=1, keepdims=True)
    stat_out[...] = jnp.where(lane == 0, mean, jnp.where(lane == 1, m2, 0.0))
    stat_copy = remote(stat_out, stat_in, st_send, st_recv, mp=other)
    stat_copy.start()
    stat_copy.wait_recv()
    mean_o = stat_in[:, 0:1]
    m2_o = stat_in[:, 1:2]
    center = (mean + mean_o) * 0.5
    gap = mean - mean_o
    var = (m2 + m2_o + gap * gap * (W * 0.5)) * (1.0 / (2 * W))
    normed = ((rows - center) * lax.rsqrt(var + EPSILON) * gain_ref[...] + bias_ref[...]).astype(BF16)
    outgoing = lax.dot_general(
        place, normed, (((0,), (0,)), ((), ())), preferred_element_type=F32
    ).astype(BF16)
    for e in range(E):
        sendbuf[e] = outgoing[e * C:(e + 1) * C]

    pending = []

    def spread(src, at, d):
        for k in range(1, DP):
            copy = remote(
                src, at, dx_send.at[k - 1, d], dx_recv.at[k - 1, d], dp=lax.rem(x + k, DP)
            )
            copy.start()
            pending.append(copy)
        copy = remote(src, at, dp_send.at[0, d], dp_recv.at[0, d], mp=other)
        copy.start()
        pending.append(copy)

    def block(half, xi, zi):
        return xbuf.at[half, xi * E + zi]

    for d in range(1, E):
        zd = lax.rem(z + d, E)
        copy = remote(
            sendbuf.at[zd], block(m, x, z), dz_send.at[d - 1], dz_recv.at[d - 1], expert=zd
        )
        copy.start()
        pending.append(copy)
    local = pltpu.make_async_copy(sendbuf.at[z], block(m, x, z), lsem.at[1])
    local.start()
    spread(sendbuf.at[z], block(m, x, z), 0)

    def landed(dst, recv):
        remote(dst, dst, st_send, recv, mp=other).wait_recv()

    for d in range(1, E):
        zs_from = lax.rem(z + E - d, E)
        mine = block(m, x, zs_from)
        landed(mine, dz_recv.at[d - 1])
        spread(mine, mine, d)
    local.wait()
    for d in range(E):
        landed(block(other, x, lax.rem(z + E - d, E)), dp_recv.at[0, d])

    copies_w[0].wait()

    TILE = 512

    def first(xi):
        left = xbuf[0, pl.ds(xi * E, E)].reshape(EC, W)
        right = xbuf[1, pl.ds(xi * E, E)].reshape(EC, W)
        rows_at = pl.ds(pl.multiple_of(xi * EC, 16), EC)

        def tile(j, carry):
            at = pl.ds(pl.multiple_of(j * TILE, TILE), TILE)
            hidden = jnp.dot(left, w1[0:W, at], preferred_element_type=F32)
            hidden = hidden + jnp.dot(right, w1[W:2 * W, at], preferred_element_type=F32)
            act[rows_at, at] = jnp.maximum(hidden, 0.0).astype(BF16)
            return carry

        lax.fori_loop(0, FFL // TILE, tile, 0)

    first(x)
    for k in range(1, DP):
        xi = lax.rem(x + DP - k, DP)
        for d in range(E):
            mine = block(m, xi, lax.rem(z + E - d, E))
            landed(mine, dx_recv.at[k - 1, d])
            copy = remote(mine, mine, dp_send.at[k, d], dp_recv.at[k, d], mp=other)
            copy.start()
            pending.append(copy)
        for d in range(E):
            landed(block(other, xi, lax.rem(z + E - d, E)), dp_recv.at[k, d])
        first(xi)

    copies_w[1].wait()
    R = DP * EC
    group = R if R <= 512 else EC

    def second(half, q, dst):
        at = pl.ds(pl.multiple_of(half * W + q * wq, wq), wq)

        def some(i, carry):
            rows_at = pl.ds(pl.multiple_of(i * group, 16), group)
            dst[q, rows_at, :] = jnp.dot(
                act[rows_at, :], w2[:, at], preferred_element_type=F32
            ).astype(BF16)
            return carry

        lax.fori_loop(0, R // group, some, 0)

    def column(xi):
        return pl.ds(pl.multiple_of(xi * EC, 16), EC)

    def reduce_mp(q):
        landed(prec.at[q], rp_recv.at[q])
        xs[q] = (pown[q].astype(F32) + prec[q].astype(F32)).astype(BF16)
        for k in range(1, DP):
            xd = lax.rem(x + k, DP)
            copy = remote(
                xs.at[q, column(xd)], xr.at[q, k - 1], rx_send.at[q, k - 1], rx_recv.at[q, k - 1], dp=xd
            )
            copy.start()
            pending.append(copy)

    for q in range(NQ):
        second(other, q, psend)
        copy = remote(psend.at[q], prec.at[q], rp_send.at[q], rp_recv.at[q], mp=other)
        copy.start()
        pending.append(copy)
        second(m, q, pown)
        if q >= 1:
            reduce_mp(q - 1)
    reduce_mp(NQ - 1)

    for q in range(NQ):
        total = xs[q, column(x), :].astype(F32)
        for k in range(1, DP):
            landed(xr.at[q, k - 1], rx_recv.at[q, k - 1])
            total = total + xr[q, k - 1].astype(F32)
        total = total.astype(BF16)
        for e in range(E):
            zs[q, e] = total[e * C:(e + 1) * C]
        for d in range(1, E):
            zd = lax.rem(z + d, E)
            copy = remote(
                zs.at[q, zd], zr.at[q, z], rz_send.at[q, d - 1], rz_recv.at[q, d - 1], expert=zd
            )
            copy.start()
            pending.append(copy)
        zr[q, pl.ds(z, 1)] = zs[q, pl.ds(z, 1)]

    for q in range(NQ):
        for d in range(1, E):
            landed(zr.at[q, lax.rem(z + E - d, E)], rz_recv.at[q, d - 1])
        back = zr[q].reshape(EC, wq)
        mixed = jnp.dot(mix_hi, back, preferred_element_type=F32)
        mixed = mixed + jnp.dot(mix_lo, back, preferred_element_type=F32)
        at = slice(q * wq, (q + 1) * wq)
        out_ref[:, at] = (att[:, at].astype(F32) + mixed).astype(BF16)

    for h in range(E - 1):
        for c in range(NC):
            for direction in range(2):
                @pl.when(sends(direction, h))
                def _():
                    hop(direction, h, c).wait_send()
    for copy in sp_copies:
        copy.wait_send()
    stat_copy.wait_send()
    for copy in pending:
        copy.wait_send()


def shards(
    hidden, queries, memory, target_pair, source_pair, routes, route_weight,
    norm_gain, norm_bias, expert_in, expert_out,
):
    E = lax.axis_size("expert")
    DP = lax.axis_size("dp")
    T, W = hidden.shape
    S = memory.shape[0]
    NC, NQ = 2, 4
    cap = 2 * T // E * 5 // 4
    C = -(-cap // 8) * 8
    cols, wq, EC = W // NC, W // NQ, E * C
    R = DP * EC
    FFL = expert_in.shape[2]
    kv = jnp.transpose(memory.reshape(S, 2, NC, cols), (2, 1, 0, 3))
    m = lax.axis_index("mp")
    gain = lax.dynamic_slice(norm_gain, (m * W,), (W,)).reshape(1, W)
    bias = lax.dynamic_slice(norm_bias, (m * W,), (W,)).reshape(1, W)
    vmem = pl.BlockSpec(memory_space=pltpu.VMEM)
    hbm = pl.BlockSpec(memory_space=pl.ANY)
    dma = pltpu.SemaphoreType.DMA
    return pl.pallas_call(
        functools.partial(layer, E, DP, NC, NQ, C),
        out_shape=jax.ShapeDtypeStruct((T, W), BF16),
        in_specs=[hbm] + [vmem] * 8 + [hbm] * 2,
        out_specs=vmem,
        scratch_shapes=[
            pltpu.VMEM((E, NC, 2, S, cols), BF16),
            pltpu.VMEM((E, 1, S), jnp.int32),
            pltpu.VMEM((2 * W, FFL), BF16),
            pltpu.VMEM((FFL, 2 * W), BF16),
            pltpu.VMEM((T, W), BF16),
            pltpu.VMEM((T, 128), F32),
            pltpu.VMEM((T, 128), F32),
            pltpu.VMEM((E, C, W), BF16),
            pltpu.VMEM((2, DP * E, C, W), BF16),
            pltpu.VMEM((R, FFL), BF16),
            pltpu.VMEM((NQ, R, wq), BF16),
            pltpu.VMEM((NQ, R, wq), BF16),
            pltpu.VMEM((NQ, R, wq), BF16),
            pltpu.VMEM((NQ, R, wq), BF16),
            pltpu.VMEM((NQ, max(DP - 1, 1), EC, wq), BF16),
            pltpu.VMEM((NQ, E, C, wq), BF16),
            pltpu.VMEM((NQ, E, C, wq), BF16),
            dma((2,)),
            dma((2,)),
            dma((2, E - 1, NC)),
            dma((2, E - 1, NC)),
            dma((E - 1,)),
            dma((E - 1,)),
            dma,
            dma,
            dma((E - 1,)),
            dma((E - 1,)),
            dma((DP - 1, E)),
            dma((DP - 1, E)),
            dma((DP, E)),
            dma((DP, E)),
            dma((NQ,)),
            dma((NQ,)),
            dma((NQ, DP - 1)),
            dma((NQ, DP - 1)),
            dma((NQ, E - 1)),
            dma((NQ, E - 1)),
        ],
        compiler_params=pltpu.CompilerParams(
            collective_id=0, has_side_effects=True, vmem_limit_bytes=60 * 1024 * 1024
        ),
    )(
        kv, source_pair.reshape(1, S), queries, hidden, target_pair.reshape(T, 1), routes, route_weight,
        gain, bias,
        expert_in.reshape(2 * W, FFL), expert_out.reshape(FFL, 2 * W),
    )


def solution(mesh):
    rows = ("groups", "expert", "dp")
    return jax.shard_map(
        shards,
        mesh=mesh,
        in_specs=(
            P(rows, "mp"),
            P(rows, "mp"),
            P(rows, None, "mp"),
            P(rows),
            P(rows),
            P(rows, None),
            P(rows, None),
            P(),
            P(),
            P("expert", None, ("dp", "mp")),
            P("expert", ("dp", "mp"), None),
        ),
        out_specs=P(rows, "mp"),
        check_vma=False,
    )
```

time: 148 us -> 72.1 us (0.49)
  blocking collectives: 82 us -> 0 us
  Pallas kernels: 0 us -> 61.8 us
  waiting for transfers between devices: 24.1 us -> 0 us
  between operations: 14.3 us -> 0.02 us
  matrix products: 13.8 us -> 0 us
  other arithmetic: 5.38 us -> 0 us
  local copies, waits for them, and re-layouts: 8.49 us -> 10.1 us
    all_to_all x2 -> x0, blocking collectives: 70.1 us -> none  [the longest x1 35.6 us: shards(): lax.all_to_all(copies, ('expert', 'dp'), split_axis=0, concat_axis=0, til...]
    pallas_call x0 -> x1, Pallas kernels: none -> 61.8 us  [shards(): pl.pallas_call(functools.partial(layer, E, DP, NC, NQ, C), out_shape=jax....]
    all_gather x1 -> x0, waiting for transfers between devices: 16.5 us -> none  [shards(): rows = lax.all_gather(memory, 'expert', axis=0, tiled=True)]
    dot_general x5 -> x0, matrix products: 13.8 us -> none  [the longest x1 11.3 us: shards(): jnp.dot(active, expert_out[0], preferred_element_type=jnp.float32)]
    unnamed x1 -> x0, blocking collectives: 9.92 us -> none
    reduce_scatter x1 -> x0, waiting for transfers between devices: 6.83 us -> none  [shards(): lax.psum_scatter(blended.astype(jnp.bfloat16), 'mp', scatter_dimension=1,...]
    slice x1 -> x0, local copies, waits for them, and re-layouts: 3.25 us -> none  [shards(): keys = rows[:, 0, :].reshape(count, local_heads, HEAD)]
    reshape x0 -> x3, local copies, waits for them, and re-layouts: none -> 3.21 us  [the longest x2 1.86 us: shards(): kv = jnp.transpose(memory.reshape(S, 2, NC, cols), (2, 1, 0, 3))]
  transfers between devices with their start and end apart: 2 -> 0, of which waited for: 2 -> 0; matrix products, arithmetic and copies ran while one was open for 3% -> 0% of each run, Pallas kernels for 0% -> 0%
where the time goes in v1:
time: 72.1 us; the launch traced here: 71.9 us
  Pallas kernels  61.8 us (86%)
  local copies, waits for them, and re-layouts  10.1 us (14%)
    pallas_call x1, Pallas kernels, shards(): pl.pallas_call(functools.partial(layer, E, DP, NC, NQ, C), out_shape=jax....  61.8 us
    unnamed x3, local copies, waits for them, and re-layouts  4.3 us
    reshape x2, local copies, waits for them, and re-layouts, shards(): kv = jnp.transpose(memory.reshape(S, 2, NC, cols), (2, 1, 0, 3))  1.86 us

profile of v1, /device:TPU:0, one launch (start us, length us, event | category | flops | bytes accessed | tf_op | source)
XLA Modules:
  0.0 71.9 jit_solution(1988720925928293481)
XLA Ops:
  0.0 1.1 %reshape.28 = bf16[64,2,2,512]{3,2,1,0:T(2,128)(2,1)S(1)} reshape(bf16[64,2,1024]{2,1,0:T(2,128)(2,1)} %param.13) | data formatting | bytes 524288 | tf_op jit(solution)/shard_map/reshape | solution.py:339
  1.1 0.7 %copy.23 = bf16[64,2,2,512]{3,0,1,2:T(8,128)(2,1)} copy(bf16[64,2,2,512]{3,2,1,0:T(2,128)(2,1)S(1)} %reshape.28) | data formatting | bytes 524288 | tf_op jit(solution)/shard_map/reshape | solution.py:339
  1.9 1.4 %copy.17.tp_ref = s32[64,1]{1,0:T(8,128)} copy(s32[64,1]{0,1:T(1,128)} %bitcast.15) | data formatting | bytes 512 | tf_op jit(solution)/shard_map/reshape | solution.py:394
  3.2 1.4 %copy.18.routes_ref = s32[64,2]{1,0:T(8,128)} copy(s32[64,2]{0,1:T(2,128)} %param.16) | data formatting | bytes 1024 | tf_op args[5]
  4.6 1.4 %copy.19.rw_ref = f32[64,2]{1,0:T(8,128)} copy(f32[64,2]{0,1:T(2,128)} %param.17) | data formatting | bytes 1024 | tf_op args[6]
  6.0 1.3 %dynamic_slice.6 = f32[1024]{0:T(1024)} dynamic-slice(f32[2048]{0:T(1024)} %param.18, s32[]{:T(128)S(6)} %select_n.4), dynamic_slice_sizes={1024} | dynamic-slice | bytes 8196 | tf_op jit(solution)/shard_map/dynamic_slice | solution.py:341
  7.2 1.3 %dynamic_slice.7 = f32[1024]{0:T(1024)} dynamic-slice(f32[2048]{0:T(1024)} %param.19, s32[]{:T(128)S(6)} %select_n.4), dynamic_slice_sizes={1024} | dynamic-slice | bytes 8196 | tf_op jit(solution)/shard_map/dynamic_slice | solution.py:342
  8.5 61.8 %shard_map.109 = bf16[64,1024]{1,0:T(8,128)(2,1)} custom-call(bf16[2,2,64,512]{3,2,1,0:T(8,128)(2,1)} %bitcast.11, s32[1,64]{1,0:T(1,128)} %bitcast.14, bf16[64,1024]{1,0:T(8,128)(2,1)} %q_ref.1, bf16[64,1024]{1,0:T(8,128)(2,1)} %hid_ref.1, s32[64,1]{1,0:T(8,128)} %copy.17.tp_ref, s32[64,2]{1,0:T(8,128)} %copy.18.routes_ref, f32[64,2]{1,0:T(8,128)} %copy.19.rw_ref, ...), custom_call_target="tpu_custom_call" | custom-call | tf_op jit(solution)/shard_map/pallas_call | solution.py:346
  70.3 1.6 %copy.25 = bf16[64,1024]{1,0:T(8,128)(2,1)} copy(bf16[64,1024]{1,0:T(8,128)(2,1)} %shard_map.109) | data formatting | bytes 262144

commit v2 on v1

--- a/solution.py
+++ b/solution.py
@@ -26,6 +26,7 @@
     E, DP, NC, NQ, C,
     kv_ref, sp_ref, q_ref, hid_ref, tp_ref, routes_ref, rw_ref, gain_ref, bias_ref, w1_hbm, w2_hbm,
     out_ref,
+    q_end, tp_end, num_out, num_in, aux_out, aux_in, near_num, end_send, end_recv, pt_send, pt_recv,
     kv, sp, w1, w2, att, stat_out, stat_in, sendbuf, xbuf, act, psend, pown, prec, xs, xr, zs, zr,
     wsem, lsem, kv_send, kv_recv, sp_send, sp_recv, st_send, st_recv,
     dz_send, dz_recv, dx_send, dx_recv, dp_send, dp_recv,
@@ -71,8 +72,30 @@
 
     def sends(direction, h):
         if direction == 0:
-            return jnp.logical_and(z >= h, z < E - 1)
-        return jnp.logical_and(z <= E - 1 - h, z > 0)
+            ok = jnp.logical_and(z >= h, z < E - 1)
+            return ok if h == 0 else jnp.logical_and(ok, z < E - 2)
+        ok = jnp.logical_and(z <= E - 1 - h, z > 0)
+        return ok if h == 0 else jnp.logical_and(ok, z > 1)
+
+    def comes(direction, h):
+        if direction == 0:
+            ok = z >= h
+            return ok if h == 1 else jnp.logical_and(ok, z < E - 1)
+        ok = z <= E - 1 - h
+        return ok if h == 1 else jnp.logical_and(ok, z > 0)
+
+    is_end = jnp.logical_or(z == 0, z == E - 1)
+    is_helper = jnp.logical_or(z == 1, z == E - 2)
+    end = jnp.where(z == 1, 0, E - 1)
+    helper = jnp.where(z == 0, 1, E - 2)
+    q_copy = remote(q_ref, q_end, end_send.at[0], end_recv.at[0], expert=helper)
+    tp_copy = remote(tp_ref, tp_end, end_send.at[1], end_recv.at[1], expert=helper)
+
+    def part_copies(c):
+        return [
+            remote(num_out.at[c], num_in.at[c], pt_send.at[0, c], pt_recv.at[0, c], expert=end),
+            remote(aux_out.at[c], aux_in.at[c], pt_send.at[1, c], pt_recv.at[1, c], expert=end),
+        ]
 
     def arrived(direction, h, c):
         owner = z - h if direction == 0 else z + h
@@ -81,24 +104,37 @@
             kv_send.at[direction, h - 1, c], kv_recv.at[direction, h - 1, c], expert=owner,
         )
 
+    sp_copies = []
+    for d in range(1, E):
+        copy = remote(
+            sp_ref, sp.at[z], sp_send.at[d - 1], sp_recv.at[d - 1], expert=lax.rem(z + d, E)
+        )
+        copy.start()
+        sp_copies.append(copy)
+    @pl.when(is_end)
+    def _():
+        tp_copy.start()
+
     for c in range(NC):
         for direction in range(2):
             @pl.when(sends(direction, 0))
             def _():
                 hop(direction, 0, c).start()
 
-    sp_copies = []
-    for d in range(1, E):
-        copy = remote(
-            sp_ref, sp.at[z], sp_send.at[d - 1], sp_recv.at[d - 1], expert=lax.rem(z + d, E)
-        )
-        copy.start()
-        sp_copies.append(copy)
+    @pl.when(is_end)
+    def _():
+        q_copy.start()
+
     for copy in copies_w:
         copy.start()
 
-    r0 = routes_ref[:, 0:1]
-    r1 = routes_ref[:, 1:2]
+    eye = lax.broadcasted_iota(jnp.int32, (T, T), 0) == lax.broadcasted_iota(jnp.int32, (T, T), 1)
+
+    def upright(row):
+        return jnp.sum(jnp.where(eye, row.astype(F32), 0.0), axis=1, keepdims=True)
+
+    r0 = upright(routes_ref[0:1, :]).astype(jnp.int32)
+    r1 = upright(routes_ref[1:2, :]).astype(jnp.int32)
     lane = lax.broadcasted_iota(jnp.int32, (T, 128), 1)
     member = jnp.logical_or(lane == r0, lane == r1).astype(F32).astype(BF16)
     tri = (
@@ -111,47 +147,112 @@
     place0 = place_lane == r0 * C + slot0
     place1 = place_lane == r1 * C + slot1
     place = jnp.logical_or(place0, place1).astype(F32).astype(BF16)
-    mixing = jnp.where(place0, rw_ref[:, 0:1], 0.0) + jnp.where(place1, rw_ref[:, 1:2], 0.0)
+    mixing = jnp.where(place0, upright(rw_ref[0:1, :]), 0.0)
+    mixing = mixing + jnp.where(place1, upright(rw_ref[1:2, :]), 0.0)
     mix_hi = mixing.astype(BF16)
     mix_lo = (mixing - mix_hi.astype(F32)).astype(BF16)
 
-    for h in range(1, E):
+    tp = upright(tp_ref[...]).astype(jnp.int32)
+    own_kv.wait()
+    for copy in sp_copies:
+        copy.wait_recv()
+    pairs = [jnp.where(j == z, sp_ref[...], sp[j]) for j in range(E)]
+    all_pairs = jnp.concatenate(pairs, axis=1)
+    scale = 1.0 / math.sqrt(HEAD)
+
+    def attend(query, keys, vals, match):
+        score = lax.dot_general(
+            query, keys, (((1,), (1,)), ((), ())), preferred_element_type=F32
+        ) * scale
+        masked = jnp.where(match, score, NEGATIVE)
+        largest = jnp.max(masked, axis=1, keepdims=True)
+        weight = jnp.where(match, jnp.exp(masked - largest), 0.0)
+        total = jnp.sum(weight, axis=1, keepdims=True)
+        return largest, total, jnp.dot(weight.astype(BF16), vals, preferred_element_type=F32)
+
+    def heads(c):
+        for n in range(cols // HEAD):
+            yield n, slice(n * HEAD, (n + 1) * HEAD), slice(c * cols + n * HEAD, c * cols + (n + 1) * HEAD)
+
+    def flat(column):
+        return jnp.sum(jnp.where(eye, column, 0.0), axis=0, keepdims=True)
+
+    def help_end(c):
+        tpe = upright(tp_end[...]).astype(jnp.int32)
+        far = jnp.concatenate(
+            [jnp.where(jnp.logical_or(j == z, j == end), -1, pairs[j]) for j in range(E)], axis=1
+        )
+        match = far == tpe
+        for n, at, full in heads(c):
+            keys = kv[:, c, 0, :, at].reshape(E * S, HEAD)
+            vals = kv[:, c, 1, :, at].reshape(E * S, HEAD)
+            largest, total, num = attend(q_end[:, full], keys, vals, match)
+            num_out[c, :, at] = num.astype(BF16)
+            aux_out[c, 2 * n:2 * n + 1, :] = flat(largest)
+            aux_out[c, 2 * n + 1:2 * n + 2, :] = flat(total)
+        for copy in part_copies(c):
+            copy.start()
+
+    for h in range(1, E - 1):
+        if h == E - 2:
+            @pl.when(is_helper)
+            def _():
+                q_copy.wait_recv()
+                tp_copy.wait_recv()
+
         for c in range(NC):
             for direction in range(2):
-                here = z >= h if direction == 0 else z <= E - 1 - h
-
-                @pl.when(here)
+                @pl.when(comes(direction, h))
                 def _():
                     arrived(direction, h, c).wait_recv()
 
-                if h < E - 1:
+                if h < E - 2:
                     @pl.when(sends(direction, h))
                     def _():
                         hop(direction, h, c).start()
-    own_kv.wait()
-    for copy in sp_copies:
-        copy.wait_recv()
-
-    tp = tp_ref[...]
-    match = jnp.concatenate(
-        [jnp.where(j == z, sp_ref[...], sp[j]) for j in range(E)], axis=1
-    ) == tp
-    scale = 1.0 / math.sqrt(HEAD)
-    for c in range(NC):
-        for n in range(cols // HEAD):
-            at = slice(n * HEAD, (n + 1) * HEAD)
-            full = slice(c * cols + n * HEAD, c * cols + (n + 1) * HEAD)
-            keys = kv[:, c, 0, :, at].reshape(E * S, HEAD)
-            vals = kv[:, c, 1, :, at].reshape(E * S, HEAD)
-            score = lax.dot_general(
-                q_ref[:, full], keys, (((1,), (1,)), ((), ())), preferred_element_type=F32
-            ) * scale
-            masked = jnp.where(match, score, NEGATIVE)
-            largest = jnp.max(masked, axis=1, keepdims=True)
-            weight = jnp.where(match, jnp.exp(masked - largest), 0.0)
-            total = jnp.sum(weight, axis=1, keepdims=True)
-            context = jnp.dot(weight.astype(BF16), vals, preferred_element_type=F32) / total
-            att[:, full] = (hid_ref[:, full].astype(F32) + context).astype(BF16)
+
+            if h == E - 2:
+                @pl.when(is_helper)
+                def _():
+                    help_end(c)
+
+    @pl.when(jnp.logical_not(is_end))
+    def _():
+        match = all_pairs == tp
+        for c in range(NC):
+            for n, at, full in heads(c):
+                keys = kv[:, c, 0, :, at].reshape(E * S, HEAD)
+                vals = kv[:, c, 1, :, at].reshape(E * S, HEAD)
+                _, total, num = attend(q_ref[:, full], keys, vals, match)
+                att[:, full] = (hid_ref[:, full].astype(F32) + num / total).astype(BF16)
+
+    @pl.when(is_end)
+    def _():
+        near = jnp.concatenate(
+            [sp_ref[...], jnp.where(z == 0, pairs[1], pairs[E - 2])], axis=1
+        )
+        match = near == tp
+        mine = []
+        for c in range(NC):
+            for n, at, full in heads(c):
+                keys = jnp.concatenate([kv[z, c, 0, :, at], kv[helper, c, 0, :, at]], axis=0)
+                vals = jnp.concatenate([kv[z, c, 1, :, at], kv[helper, c, 1, :, at]], axis=0)
+                largest, total, num = attend(q_ref[:, full], keys, vals, match)
+                near_num[:, full] = num
+                mine.append((largest, total))
+        for c in range(NC):
+            for copy in part_copies(c):
+                copy.wait_recv()
+            for n, at, full in heads(c):
+                largest, total = mine[c * (cols // HEAD) + n]
+                largest_far = upright(aux_in[c, 2 * n:2 * n + 1, :])
+                total_far = upright(aux_in[c, 2 * n + 1:2 * n + 2, :])
+                top = jnp.maximum(largest, largest_far)
+                near_scale = jnp.exp(largest - top)
+                far_scale = jnp.exp(largest_far - top)
+                num = near_num[:, full] * near_scale + num_in[c, :, at].astype(F32) * far_scale
+                context = num / (total * near_scale + total_far * far_scale)
+                att[:, full] = (hid_ref[:, full].astype(F32) + context).astype(BF16)
 
     rows = att[...].astype(F32)
     mean = jnp.mean(rows, axis=1, keepdims=True)
@@ -166,7 +267,10 @@
     center = (mean + mean_o) * 0.5
     gap = mean - mean_o
     var = (m2 + m2_o + gap * gap * (W * 0.5)) * (1.0 / (2 * W))
-    normed = ((rows - center) * lax.rsqrt(var + EPSILON) * gain_ref[...] + bias_ref[...]).astype(BF16)
+    half_at = pl.ds(pl.multiple_of(m * W, 128), W)
+    gain = gain_ref[:, half_at]
+    bias = bias_ref[:, half_at]
+    normed = ((rows - center) * lax.rsqrt(var + EPSILON) * gain + bias).astype(BF16)
     outgoing = lax.dot_general(
         place, normed, (((0,), (0,)), ((), ())), preferred_element_type=F32
     ).astype(BF16)
@@ -244,29 +348,35 @@
         first(xi)
 
     copies_w[1].wait()
-    R = DP * EC
-    group = R if R <= 512 else EC
-
-    def second(half, q, dst):
-        at = pl.ds(pl.multiple_of(half * W + q * wq, wq), wq)
-
-        def some(i, carry):
-            rows_at = pl.ds(pl.multiple_of(i * group, 16), group)
-            dst[q, rows_at, :] = jnp.dot(
-                act[rows_at, :], w2[:, at], preferred_element_type=F32
-            ).astype(BF16)
-            return carry
-
-        lax.fori_loop(0, R // group, some, 0)
-
     def column(xi):
         return pl.ds(pl.multiple_of(xi * EC, 16), EC)
 
-    def reduce_mp(q):
-        landed(prec.at[q], rp_recv.at[q])
-        xs[q] = (pown[q].astype(F32) + prec[q].astype(F32)).astype(BF16)
+    def second(half, q, xi, dst):
+        at = pl.ds(pl.multiple_of(half * W + q * wq, wq), wq)
+        dst[q, column(xi), :] = jnp.dot(
+            act[column(xi), :], w2[:, at], preferred_element_type=F32
+        ).astype(BF16)
+
+    def swap(q, k):
+        xi = lax.rem(x + k, DP)
+        second(other, q, xi, psend)
+        copy = remote(
+            psend.at[q, column(xi)], prec.at[q, column(xi)],
+            rp_send.at[q, k], rp_recv.at[q, k], mp=other,
+        )
+        copy.start()
+        pending.append(copy)
+        second(m, q, xi, pown)
+
+    def both(q, k):
+        xi = lax.rem(x + k, DP)
+        landed(prec.at[q, column(xi)], rp_recv.at[q, k])
+        return pown[q, column(xi), :].astype(F32) + prec[q, column(xi), :].astype(F32)
+
+    def pass_on(q):
         for k in range(1, DP):
             xd = lax.rem(x + k, DP)
+            xs[q, column(xd), :] = both(q, k).astype(BF16)
             copy = remote(
                 xs.at[q, column(xd)], xr.at[q, k - 1], rx_send.at[q, k - 1], rx_recv.at[q, k - 1], dp=xd
             )
@@ -274,17 +384,17 @@
             pending.append(copy)
 
     for q in range(NQ):
-        second(other, q, psend)
-        copy = remote(psend.at[q], prec.at[q], rp_send.at[q], rp_recv.at[q], mp=other)
-        copy.start()
-        pending.append(copy)
-        second(m, q, pown)
+        for k in range(1, DP):
+            swap(q, k)
         if q >= 1:
-            reduce_mp(q - 1)
-    reduce_mp(NQ - 1)
+            pass_on(q - 1)
+    pass_on(NQ - 1)
 
     for q in range(NQ):
-        total = xs[q, column(x), :].astype(F32)
+        swap(q, 0)
+
+    for q in range(NQ):
+        total = both(q, 0)
         for k in range(1, DP):
             landed(xr.at[q, k - 1], rx_recv.at[q, k - 1])
             total = total + xr[q, k - 1].astype(F32)
@@ -315,6 +425,17 @@
                 @pl.when(sends(direction, h))
                 def _():
                     hop(direction, h, c).wait_send()
+    @pl.when(is_end)
+    def _():
+        q_copy.wait_send()
+        tp_copy.wait_send()
+
+    @pl.when(is_helper)
+    def _():
+        for c in range(NC):
+            for copy in part_copies(c):
+                copy.wait_send()
+
     for copy in sp_copies:
         copy.wait_send()
     stat_copy.wait_send()
@@ -330,16 +451,13 @@
     DP = lax.axis_size("dp")
     T, W = hidden.shape
     S = memory.shape[0]
-    NC, NQ = 2, 4
+    NC, NQ = 4, 4
     cap = 2 * T // E * 5 // 4
     C = -(-cap // 8) * 8
     cols, wq, EC = W // NC, W // NQ, E * C
     R = DP * EC
     FFL = expert_in.shape[2]
     kv = jnp.transpose(memory.reshape(S, 2, NC, cols), (2, 1, 0, 3))
-    m = lax.axis_index("mp")
-    gain = lax.dynamic_slice(norm_gain, (m * W,), (W,)).reshape(1, W)
-    bias = lax.dynamic_slice(norm_bias, (m * W,), (W,)).reshape(1, W)
     vmem = pl.BlockSpec(memory_space=pltpu.VMEM)
     hbm = pl.BlockSpec(memory_space=pl.ANY)
     dma = pltpu.SemaphoreType.DMA
@@ -349,6 +467,17 @@
         in_specs=[hbm] + [vmem] * 8 + [hbm] * 2,
         out_specs=vmem,
         scratch_shapes=[
+            pltpu.VMEM((T, W), BF16),
+            pltpu.VMEM((1, T), jnp.int32),
+            pltpu.VMEM((NC, T, cols), BF16),
+            pltpu.VMEM((NC, T, cols), BF16),
+            pltpu.VMEM((NC, 8, T), F32),
+            pltpu.VMEM((NC, 8, T), F32),
+            pltpu.VMEM((T, W), F32),
+            dma((2,)),
+            dma((2,)),
+            dma((2, NC)),
+            dma((2, NC)),
             pltpu.VMEM((E, NC, 2, S, cols), BF16),
             pltpu.VMEM((E, 1, S), jnp.int32),
             pltpu.VMEM((2 * W, FFL), BF16),
@@ -380,8 +509,8 @@
             dma((DP - 1, E)),
             dma((DP, E)),
             dma((DP, E)),
-            dma((NQ,)),
-            dma((NQ,)),
+            dma((NQ, DP)),
+            dma((NQ, DP)),
             dma((NQ, DP - 1)),
             dma((NQ, DP - 1)),
             dma((NQ, E - 1)),
@@ -391,8 +520,8 @@
             collective_id=0, has_side_effects=True, vmem_limit_bytes=60 * 1024 * 1024
         ),
     )(
-        kv, source_pair.reshape(1, S), queries, hidden, target_pair.reshape(T, 1), routes, route_weight,
-        gain, bias,
+        kv, source_pair.reshape(1, S), queries, hidden, target_pair.reshape(1, T), routes.T, route_weight.T,
+        norm_gain.reshape(1, 2 * W), norm_bias.reshape(1, 2 * W),
         expert_in.reshape(2 * W, FFL), expert_out.reshape(FFL, 2 * W),
     )
 

time: 72.1 us -> 60.1 us (0.83)
  local copies, waits for them, and re-layouts: 10.1 us -> 3.43 us
  Pallas kernels: 61.8 us -> 56.5 us
    pallas_call x1, Pallas kernels: 61.8 us -> 56.5 us  [shards(): pl.pallas_call(functools.partial(layer, E, DP, NC, NQ, C), out_shape=jax....]
    unnamed x3 -> x1, local copies, waits for them, and re-layouts: 4.3 us -> 1.57 us
    dynamic_slice x2 -> x0, local copies, waits for them, and re-layouts: 2.55 us -> none  [the longest x1 1.28 us: shards(): bias = lax.dynamic_slice(norm_bias, (m * W,), (W,)).reshape(1, W)]
    reshape x1 -> x0, local copies, waits for them, and re-layouts: 1.36 us -> none  [shards(): target_pair.reshape(T, 1)]
where the time goes in v2:
time: 60.1 us; the launch traced here: 60 us
  Pallas kernels  56.5 us (94%)
  local copies, waits for them, and re-layouts  3.43 us (6%)
    pallas_call x1, Pallas kernels, shards(): pl.pallas_call(functools.partial(layer, E, DP, NC, NQ, C), out_shape=jax....  56.5 us
    reshape x2, local copies, waits for them, and re-layouts, shards(): kv = jnp.transpose(memory.reshape(S, 2, NC, cols), (2, 1, 0, 3))  1.86 us
    unnamed x1, local copies, waits for them, and re-layouts  1.57 us

profile of v2, /device:TPU:0, one launch (start us, length us, event | category | flops | bytes accessed | tf_op | source)
XLA Modules:
  0.0 60.0 jit_solution(3424346939985301834)
XLA Ops:
  0.0 1.1 %reshape.28 = bf16[64,2,4,256]{3,2,1,0:T(4,128)(2,1)S(1)} reshape(bf16[64,2,1024]{2,1,0:T(2,128)(2,1)} %param.13) | data formatting | bytes 524288 | tf_op jit(solution)/shard_map/reshape | solution.py:460
  1.1 0.7 %copy.17 = bf16[64,2,4,256]{3,0,1,2:T(8,128)(2,1)} copy(bf16[64,2,4,256]{3,2,1,0:T(4,128)(2,1)S(1)} %reshape.28) | data formatting | bytes 524288 | tf_op jit(solution)/shard_map/reshape | solution.py:460
  1.9 56.5 %shard_map.109 = bf16[64,1024]{1,0:T(8,128)(2,1)} custom-call(bf16[4,2,64,256]{3,2,1,0:T(8,128)(2,1)} %bitcast.13, s32[1,64]{1,0:T(1,128)} %bitcast.18, bf16[64,1024]{1,0:T(8,128)(2,1)} %q_ref.1, bf16[64,1024]{1,0:T(8,128)(2,1)} %hid_ref.1, s32[1,64]{1,0:T(1,128)} %bitcast.19, s32[2,64]{1,0:T(2,128)} %bitcast.16, f32[2,64]{1,0:T(2,128)} %bitcast.17, ...), custom_call_target="tpu_custom_call" | custom-call | tf_op jit(solution)/shard_map/pallas_call | solution.py:464
  58.4 1.6 %copy.19 = bf16[64,1024]{1,0:T(8,128)(2,1)} copy(bf16[64,1024]{1,0:T(8,128)(2,1)} %shard_map.109) | data formatting | bytes 262144

commit v3 on v2

--- a/solution.py
+++ b/solution.py
@@ -24,9 +24,9 @@
 
 def layer(
     E, DP, NC, NQ, C,
-    kv_ref, sp_ref, q_ref, hid_ref, tp_ref, routes_ref, rw_ref, gain_ref, bias_ref, w1_hbm, w2_hbm,
+    kv_ref, sp_ref, q_hbm, hid_hbm, tp_ref, routes_ref, rw_ref, gain_ref, bias_ref, w1_hbm, w2_hbm,
     out_ref,
-    q_end, tp_end, num_out, num_in, aux_out, aux_in, near_num, end_send, end_recv, pt_send, pt_recv,
+    q_ref, hid_ref, q_end, tp_end, num_out, num_in, aux_out, aux_in, near_num, end_send, end_recv, pt_send, pt_recv, own_sem,
     kv, sp, w1, w2, att, stat_out, stat_in, sendbuf, xbuf, act, psend, pown, prec, xs, xr, zs, zr,
     wsem, lsem, kv_send, kv_recv, sp_send, sp_recv, st_send, st_recv,
     dz_send, dz_recv, dx_send, dx_recv, dp_send, dp_recv,
@@ -47,8 +47,16 @@
         pltpu.make_async_copy(w1_hbm, w1, wsem.at[0]),
         pltpu.make_async_copy(w2_hbm, w2, wsem.at[1]),
     ]
-    own_kv = pltpu.make_async_copy(kv_ref, kv.at[z], lsem.at[0])
-    own_kv.start()
+    def own_block(c):
+        return kv_ref.at[:, :, pl.ds(c * cols, cols)]
+
+    own_kv = [pltpu.make_async_copy(own_block(c), kv.at[z, c], own_sem.at[c]) for c in range(NC)]
+    for copy in own_kv:
+        copy.start()
+    q_in = pltpu.make_async_copy(q_hbm, q_ref, lsem.at[0])
+    hid_in = pltpu.make_async_copy(hid_hbm, hid_ref, wsem.at[2])
+    q_in.start()
+    hid_in.start()
 
     barrier = pltpu.get_barrier_semaphore()
     for d in range(1, E):
@@ -65,7 +73,7 @@
     def hop(direction, h, c):
         owner = z - h if direction == 0 else z + h
         target = z + 1 if direction == 0 else z - 1
-        src = kv_ref.at[c] if h == 0 else kv.at[owner, c]
+        src = own_block(c) if h == 0 else kv.at[owner, c]
         return remote(
             src, kv.at[owner, c], kv_send.at[direction, h, c], kv_recv.at[direction, h, c], expert=target
         )
@@ -88,7 +96,7 @@
     is_helper = jnp.logical_or(z == 1, z == E - 2)
     end = jnp.where(z == 1, 0, E - 1)
     helper = jnp.where(z == 0, 1, E - 2)
-    q_copy = remote(q_ref, q_end, end_send.at[0], end_recv.at[0], expert=helper)
+    q_copy = remote(q_hbm, q_end, end_send.at[0], end_recv.at[0], expert=helper)
     tp_copy = remote(tp_ref, tp_end, end_send.at[1], end_recv.at[1], expert=helper)
 
     def part_copies(c):
@@ -153,7 +161,10 @@
     mix_lo = (mixing - mix_hi.astype(F32)).astype(BF16)
 
     tp = upright(tp_ref[...]).astype(jnp.int32)
-    own_kv.wait()
+    for copy in own_kv:
+        copy.wait()
+    q_in.wait()
+    hid_in.wait()
     for copy in sp_copies:
         copy.wait_recv()
     pairs = [jnp.where(j == z, sp_ref[...], sp[j]) for j in range(E)]
@@ -457,16 +468,18 @@
     cols, wq, EC = W // NC, W // NQ, E * C
     R = DP * EC
     FFL = expert_in.shape[2]
-    kv = jnp.transpose(memory.reshape(S, 2, NC, cols), (2, 1, 0, 3))
+    kv = jnp.transpose(memory, (1, 0, 2))
     vmem = pl.BlockSpec(memory_space=pltpu.VMEM)
     hbm = pl.BlockSpec(memory_space=pl.ANY)
     dma = pltpu.SemaphoreType.DMA
     return pl.pallas_call(
         functools.partial(layer, E, DP, NC, NQ, C),
         out_shape=jax.ShapeDtypeStruct((T, W), BF16),
-        in_specs=[hbm] + [vmem] * 8 + [hbm] * 2,
+        in_specs=[hbm, vmem, hbm, hbm] + [vmem] * 5 + [hbm] * 2,
         out_specs=vmem,
         scratch_shapes=[
+            pltpu.VMEM((T, W), BF16),
+            pltpu.VMEM((T, W), BF16),
             pltpu.VMEM((T, W), BF16),
             pltpu.VMEM((1, T), jnp.int32),
             pltpu.VMEM((NC, T, cols), BF16),
@@ -478,6 +491,7 @@
             dma((2,)),
             dma((2, NC)),
             dma((2, NC)),
+            dma((NC,)),
             pltpu.VMEM((E, NC, 2, S, cols), BF16),
             pltpu.VMEM((E, 1, S), jnp.int32),
             pltpu.VMEM((2 * W, FFL), BF16),
@@ -495,7 +509,7 @@
             pltpu.VMEM((NQ, max(DP - 1, 1), EC, wq), BF16),
             pltpu.VMEM((NQ, E, C, wq), BF16),
             pltpu.VMEM((NQ, E, C, wq), BF16),
-            dma((2,)),
+            dma((3,)),
             dma((2,)),
             dma((2, E - 1, NC)),
             dma((2, E - 1, NC)),

time: 60.1 us -> 59.8 us (level)
    reshape x2 -> x0, local copies, waits for them, and re-layouts: 1.86 us -> none  [shards(): kv = jnp.transpose(memory.reshape(S, 2, NC, cols), (2, 1, 0, 3))]
    unnamed x1 -> x2, local copies, waits for them, and re-layouts: 1.57 us -> 3.26 us
where the time goes in v3:
time: 59.8 us; the launch traced here: 59.6 us
  Pallas kernels  56.3 us (94%)
  local copies, waits for them, and re-layouts  3.26 us (5%)
    pallas_call x1, Pallas kernels, shards(): pl.pallas_call(functools.partial(layer, E, DP, NC, NQ, C), out_shape=jax....  56.3 us
    unnamed x2, local copies, waits for them, and re-layouts  3.26 us

profile of v3, /device:TPU:0, one launch (start us, length us, event | category | flops | bytes accessed | tf_op | source)
XLA Modules:
  0.0 59.6 jit_solution(13869959141730009010)
XLA Ops:
  0.0 1.7 %copy.14 = bf16[64,2,1024]{2,0,1:T(8,128)(2,1)} copy(bf16[64,2,1024]{2,1,0:T(2,128)(2,1)} %param.13) | data formatting | bytes 524288 | tf_op args[2]
  1.7 56.3 %shard_map.109 = bf16[64,1024]{1,0:T(8,128)(2,1)} custom-call(bf16[2,64,1024]{2,1,0:T(8,128)(2,1)} %bitcast.13, s32[1,64]{1,0:T(1,128)} %bitcast.18, bf16[64,1024]{1,0:T(8,128)(2,1)} %q_hbm.1, bf16[64,1024]{1,0:T(8,128)(2,1)} %hid_hbm.1, s32[1,64]{1,0:T(1,128)} %bitcast.19, s32[2,64]{1,0:T(2,128)} %bitcast.16, f32[2,64]{1,0:T(2,128)} %bitcast.17, ...), custom_call_target="tpu_custom_call" | custom-call | tf_op jit(solution)/shard_map/pallas_call | solution.py:475
  58.0 1.6 %copy.16 = bf16[64,1024]{1,0:T(8,128)(2,1)} copy(bf16[64,1024]{1,0:T(8,128)(2,1)} %shard_map.109) | data formatting | bytes 262144
